TPU v7x, 128 devices: a whole 4x4x4 slice. The times are simulated.
128 devices in a mesh: dp: 16 (over y_hi, z, core), cache: 8 (over y_lo, x).
Axes of the slice: x: 4, y: 4 (y_hi: 2, y_lo: 2; y = y_hi * 2 + y_lo), z: 4, core: 2. Of those that a mesh axis runs over, the one named last changes fastest.
Arguments:
- hidden_in: bfloat16 [16384, 2560], P(('dp', 'cache')), may hold values from -6 to 6
- placing: int32 [16384], P('dp'), may hold values from 0 to 16383, as said below
- prompt_start: int32 [16384], P(('dp', 'cache')), may hold values from 0 to 16383, as said below
- attn_gain: float32 [2560], replicated, may hold values from 0.5 to 1.5
- w_qkv: bfloat16 [2560, 1792], P(('dp', 'cache'))
- w_out: bfloat16 [1280, 2560], P(('dp', 'cache')), may hold values from -0.15625 to 0.15625
- moe_gain: float32 [2560], replicated, may hold values from 0.5 to 1.5
- routes: int32 [16384, 6], P(('dp', 'cache')), may hold values from 0 to 63, all different within a row; in each aligned block of 128 rows (0 to 127, 128 to 255, ...) at most 16 rows name the same one
- route_weight: float32 [16384, 6], P(('dp', 'cache')), may hold values from 0.05 to 0.35
- w_gate_up: bfloat16 [128, 2560, 1536], P(('dp', 'cache')), may hold values from -0.125 to 0.125
- w_down: bfloat16 [128, 768, 2560], P(('dp', 'cache')), may hold values from -0.15625 to 0.15625
Outputs:
- mixed: bfloat16 [16384, 2560], P(('dp', 'cache'))
- cache_keys: bfloat16 [16384, 256], P(('dp', 'cache'))
- cache_values: bfloat16 [16384, 256], P(('dp', 'cache'))
Inputs may be any that keep to these rules, and one draw needn't show every extreme that they name: `placing`: a permutation of the 16384 positions; dealt rows g * 1024 to (g+1) * 1024 - 1 hold natural positions of the same range, and the dealt rows c * 128 + j * 16 to c * 128 + (j+1) * 16 - 1 of a group hold natural positions of its span j * 128 to (j+1) * 128 - 1. Prompts are runs of consecutive natural positions inside one group of 1024, of at most 512 tokens, some of exactly 512; prompt_start[r] <= placing[r] and it is the first position of that run. `routes`: in the rows of one device (aligned blocks of 128 rows) no expert is named more than 16 times.
All inputs are finite; a program needn't handle non-finite values.
Results may differ from a plain program's by a relative error of at most 0.014.
Values may be sent and summed in bfloat16 or wider, within the bound.
No kernel may reach another device: no remote copies, remote signals or barrier semaphores. Data moves between devices by JAX's collectives and lax.ppermute only.
A program may use at most 128 MiB of HBM per device.

v0:
```python
import jax
import jax.numpy as jnp
from jax import lax
from jax.sharding import PartitionSpec as P

HD = 128
QH = 10
KVH = 2
TOP = 6
norm_eps = 1e-05
rope_base = 500000.0
masked_score = -1e30


def rms_scaled(features, gain_vector):
    widened = features.astype(jnp.float32)
    factor = lax.rsqrt(jnp.mean(widened * widened, axis=-1, keepdims=True) + norm_eps)
    return (widened * factor * gain_vector).astype(jnp.bfloat16)


def rotated(projected, position, head_count):
    row_count = projected.shape[0]
    grouped = projected.reshape(row_count, head_count, HD)
    half_size = HD // 2
    inverse = rope_base ** (-(jnp.arange(half_size, dtype=jnp.float32) * 2.0 / HD))
    angles = position.astype(jnp.float32)[:, None] * inverse[None, :]
    cosine = jnp.cos(angles)[:, None, :]
    sine_part = jnp.sin(angles)[:, None, :]
    first_half = grouped[..., :half_size]
    second = grouped[..., half_size:]
    turned = jnp.concatenate(
        [first_half * cosine - second * sine_part, second * cosine + first_half * sine_part],
        axis=-1,
    )
    return turned.reshape(row_count, head_count * HD).astype(jnp.bfloat16)


def expert_half(slot_block, gate_up, down_part):
    flat_rows = slot_block.reshape(-1, slot_block.shape[-1])
    joined = jnp.dot(flat_rows, gate_up, preferred_element_type=jnp.float32)
    half_size = gate_up.shape[1] // 2
    active = (jax.nn.silu(joined[:, :half_size]) * joined[:, half_size:]).astype(jnp.bfloat16)
    return (
        jnp.dot(active, down_part, preferred_element_type=jnp.float32)
        .astype(jnp.bfloat16)
        .reshape(slot_block.shape)
    )


def per_device(
    hidden_in,
    placing,
    prompt_start,
    attn_gain,
    w_qkv,
    w_out,
    moe_gain,
    routes,
    route_weight,
    w_gate_up,
    w_down,
):
    row_count = hidden_in.shape[0]
    model_width = hidden_in.shape[1]
    cache_size = lax.axis_size("cache")
    my_index = lax.axis_index("cache")
    deal_rows = row_count // cache_size
    query_width = QH * HD
    kv_width = KVH * HD
    group_base = lax.axis_index("dp") * placing.shape[0]
    my_place = lax.dynamic_slice_in_dim(placing, my_index * row_count, row_count)
    position = my_place - prompt_start
    normed = rms_scaled(hidden_in, attn_gain)
    full_qkv, full_out = (
        lax.all_gather(w_qkv, ("dp", "cache"), axis=0, tiled=True),
        lax.all_gather(w_out, ("dp", "cache"), axis=0, tiled=True),
    )
    projected = jnp.dot(normed, full_qkv, preferred_element_type=jnp.float32)
    queries = rotated(projected[:, :query_width], position, QH)
    keys_here = rotated(projected[:, query_width : query_width + kv_width], position, KVH)
    values_here = projected[:, query_width + kv_width :].astype(jnp.bfloat16)
    group_size = QH // KVH
    query_heads = queries.reshape(row_count, KVH, group_size, HD)
    score_scale = HD ** (-0.5)
    highest = jnp.full((row_count, KVH, group_size), masked_score, jnp.float32)
    key_piece = lax.all_gather(keys_here, "cache", axis=0, tiled=True)
    value_piece = lax.all_gather(values_here, "cache", axis=0, tiled=True)
    piece_rows = key_piece.shape[0]
    key_heads = key_piece.reshape(piece_rows, KVH, HD)
    value_heads = value_piece.reshape(piece_rows, KVH, HD)
    scores = (
        jnp.einsum("tkgd,rkd->tkgr", query_heads, key_heads, preferred_element_type=jnp.float32)
        * score_scale
    )
    allowed = (placing[None, :] >= prompt_start[:, None]) & (placing[None, :] <= my_place[:, None])
    allowed = allowed[:, None, None, :]
    new_highest = jnp.maximum(highest, jnp.max(jnp.where(allowed, scores, masked_score), axis=-1))
    weights = jnp.where(allowed, jnp.exp(scores - new_highest[..., None]), 0.0)
    denominator = jnp.sum(weights, axis=-1)
    numerator = jnp.einsum(
        "tkgr,rkd->tkgd",
        weights.astype(jnp.bfloat16),
        value_heads,
        preferred_element_type=jnp.float32,
    )
    highest, denominator, numerator = (new_highest, denominator, numerator)
    context = (
        (numerator / denominator[..., None]).reshape(row_count, query_width).astype(jnp.bfloat16)
    )
    attn_out = jnp.dot(context, full_out, preferred_element_type=jnp.float32)
    attended = (hidden_in.astype(jnp.float32) + attn_out).astype(jnp.bfloat16)
    moe_in = rms_scaled(attended, moe_gain)
    device_count = lax.axis_size(("dp", "cache"))
    expert_count = device_count // 2
    capacity = 4 * row_count * TOP // (3 * expert_count)
    expert_ids = routes.reshape(-1)
    one_hot = (expert_ids[:, None] == jnp.arange(expert_count, dtype=jnp.int32)[None, :]).astype(
        jnp.int32
    )
    slot_rank = jnp.sum((jnp.cumsum(one_hot, axis=0) - one_hot) * one_hot, axis=1)
    slot_index = expert_ids * capacity + slot_rank
    source_row = (
        jnp.full((expert_count * capacity,), row_count, jnp.int32)
        .at[slot_index]
        .set(jnp.arange(row_count * TOP, dtype=jnp.int32) // TOP)
    )
    padded = jnp.concatenate([moe_in, jnp.zeros((1, model_width), jnp.bfloat16)], axis=0)
    outgoing = padded[source_row].reshape(expert_count, capacity, model_width)
    partial_value = expert_half(
        lax.all_to_all(
            jnp.repeat(outgoing, 2, axis=0),
            ("dp", "cache"),
            split_axis=0,
            concat_axis=0,
            tiled=True,
        ),
        w_gate_up[0],
        w_down[0],
    )
    returned = lax.all_to_all(
        partial_value, ("dp", "cache"), split_axis=0, concat_axis=0, tiled=True
    )
    halves = returned.reshape(expert_count, 2, capacity, model_width).astype(jnp.float32)
    merged = (halves[:, 0] + halves[:, 1]).astype(jnp.bfloat16)
    picked = merged.reshape(expert_count * capacity, model_width)[slot_index].reshape(
        row_count, TOP, model_width
    )
    mixture = jnp.sum(route_weight[:, :, None] * picked.astype(jnp.float32), axis=1)
    finished = (attended.astype(jnp.float32) + mixture).astype(jnp.bfloat16)
    package = (
        finished.reshape(cache_size, deal_rows, model_width),
        keys_here.reshape(cache_size, deal_rows, kv_width),
        values_here.reshape(cache_size, deal_rows, kv_width),
    )
    home_rows, home_keys, home_values = (
        lax.all_to_all(package[0], "cache", split_axis=0, concat_axis=0, tiled=True),
        lax.all_to_all(package[1], "cache", split_axis=0, concat_axis=0, tiled=True),
        lax.all_to_all(package[2], "cache", split_axis=0, concat_axis=0, tiled=True),
    )
    sender_rows = (
        jnp.arange(cache_size, dtype=jnp.int32)[:, None] * row_count
        + my_index * deal_rows
        + jnp.arange(deal_rows, dtype=jnp.int32)[None, :]
    ).reshape(-1)
    target = placing[sender_rows] - group_base - my_index * row_count
    mixed = (
        jnp.zeros((row_count, model_width), jnp.bfloat16)
        .at[target]
        .set(home_rows.reshape(-1, model_width))
    )
    cache_keys = (
        jnp.zeros((row_count, kv_width), jnp.bfloat16)
        .at[target]
        .set(home_keys.reshape(-1, kv_width))
    )
    cache_values = (
        jnp.zeros((row_count, kv_width), jnp.bfloat16)
        .at[target]
        .set(home_values.reshape(-1, kv_width))
    )
    return (mixed, cache_keys, cache_values)


def solution(mesh):
    in_specs = (
        P(("dp", "cache"), None),
        P("dp"),
        P(("dp", "cache")),
        P(),
        P(("dp", "cache"), None),
        P(("dp", "cache"), None),
        P(),
        P(("dp", "cache"), None),
        P(("dp", "cache"), None),
        P(("dp", "cache"), None, None),
        P(("dp", "cache"), None, None),
    )
    out_specs = (P(("dp", "cache"), None), P(("dp", "cache"), None), P(("dp", "cache"), None))
    return jax.shard_map(
        per_device, mesh=mesh, in_specs=in_specs, out_specs=out_specs, check_vma=False
    )
```

profile of v0, /device:TPU:33, one launch (start us, length us, event | category | flops | bytes accessed | tf_op | source)
XLA Modules:
  0.0 1172.3 jit_solution(6544326137829235413)
XLA Ops:
  7.2 0.7 all-gather.7.cloned.1.call-update
  7.9 0.7 all-gather.5.cloned.1.call-update
  8.7 0.8 copy.45
  9.7 0.8 subtract_convert_fusion.1
  10.9 0.7 broadcast_multiply_fusion
  11.9 1.8 reduce-window.6
  13.7 0.3 slice_reduce_fusion
  14.2 3.4 scatter_custom_fusion
  17.6 1.3 fusion.18
  18.9 0.9 compare_and_fusion
  19.8 310.8 %all-gather.7.cloned.1.call-done = bf16[128,10,2560]{2,1,0:T(8,128)(2,1)} async-done(((bf16[1,10,2560]{2,1,0:T(8,128)(2,1)}), bf16[128,10,2560]{2,1,0:T(8,128)(2,1)}) %all-gather.7.cloned.1.call-update) | async-done | bytes 6553616 | tf_op jit(solution)/shard_map/all_gather | solution.py:76
  330.6 12.8 %reshape.368 = bf16[1280,2560]{1,0:T(8,128)(2,1)} reshape(bf16[128,10,2560]{2,1,0:T(8,128)(2,1)} %all-gather.7.cloned.1.call-done) | data formatting | bytes 13107200
  343.4 308.3 %all-gather.5.cloned.1.call-done = bf16[128,20,1792]{2,1,0:T(8,128)(2,1)} async-done(((bf16[1,20,1792]{2,1,0:T(8,128)(2,1)}), bf16[128,20,1792]{2,1,0:T(8,128)(2,1)}) %all-gather.5.cloned.1.call-update) | async-done | bytes 9175056 | tf_op jit(solution)/shard_map/all_gather | solution.py:75
  651.7 13.2 %reshape.366 = bf16[2560,1792]{1,0:T(8,128)(2,1)} reshape(bf16[128,20,1792]{2,1,0:T(8,128)(2,1)} %all-gather.5.cloned.1.call-done) | data formatting | bytes 18350080
  664.9 5.0 fusion.30
  669.9 0.6 slice.95
  670.6 23.6 %all_gather.13 = bf16[1024,256]{1,0:T(8,128)(2,1)S(1)} all-gather(bf16[128,256]{1,0:T(8,128)(2,1)} %slice.95), channel_id=1, replica_groups=mesh['dp'=16,'cache'=8] {'cache'}, dimensions={0}, use_global_device_ids=true | all-gather | bytes 589824 | tf_op jit(solution)/shard_map/all_gather | solution.py:87
  694.5 0.3 multiply_subtract_fusion
  695.1 21.1 %all_gather.14 = bf16[1024,256]{0,1:T(8,128)(2,1)S(1)} all-gather(bf16[128,256]{0,1:T(8,128)(2,1)S(1)} %bitcast.117), channel_id=1, replica_groups=mesh['dp'=16,'cache'=8] {'cache'}, dimensions={0}, use_global_device_ids=true | all-gather | bytes 589824 | tf_op jit(solution)/shard_map/all_gather | solution.py:86
  716.2 0.2 copy.38
  716.6 1.0 fusion.5
  717.6 1.1 fusion.8
  718.7 1.1 fusion.27
  719.9 1.2 slice-done.1
  721.0 1.1 multiply_reduce_fusion.1
  722.4 6.3 gather_fusion.1
  728.8 7.8 broadcast_in_dim.35
  736.5 136.7 %all_to_all.25 = bf16[128,16,2560]{2,1,0:T(8,128)(2,1)S(1)} all-to-all(bf16[128,16,2560]{2,1,0:T(8,128)(2,1)} %bitcast.107), channel_id=1, replica_groups=mesh['dp'=16,'cache'=8] {'dp','cache'}, dimensions={0} | all-to-all | bytes 20971520 | tf_op jit(solution)/shard_map/all_to_all | solution.py:130
  873.3 21.6 %fusion.2 = f32[2048,1536]{1,0:T(8,128)} fusion(bf16[2048,2560]{1,0:T(8,128)(2,1)S(1)} %bitcast.110, bf16[1,2560,1536]{2,1,0:T(8,128)(2,1)} %param.20), kind=kOutput, calls=%fused_computation.13 | convolution fusion | flops 16106127360 | bytes 30932992 | tf_op jit(solution)/shard_map/dot_general | solution.py:40
  894.9 17.3 %convolution_convert_fusion = bf16[2048,2560]{1,0:T(8,128)(2,1)} fusion(bf16[1,768,2560]{2,1,0:T(8,128)(2,1)S(1)} %copy-done.5, f32[2048,1536]{1,0:T(8,128)} %fusion.2), kind=kOutput, calls=%fused_computation.7 | convolution fusion | flops 8067743744 | bytes 27000832 | tf_op jit(solution)/shard_map/dot_general | solution.py:44
  912.2 12.0 %all-to-all-start.1 = ((bf16[128,16,2560]{2,1,0:T(8,128)(2,1)}), bf16[128,16,2560]{2,1,0:T(8,128)(2,1)}, u32[]{:S(2)}, u32[]{:S(2)}) async-start(bf16[128,16,2560]{2,1,0:T(8,128)(2,1)} %bitcast.109), calls=%async_computation.1 | async-start | bytes 20971520 | tf_op jit(solution)/shard_map/all_to_all | solution.py:140
  924.4 0.7 convert_element_type.104
  925.1 141.6 %all-to-all-done.1 = bf16[128,16,2560]{2,1,0:T(8,128)(2,1)} async-done(((bf16[128,16,2560]{2,1,0:T(8,128)(2,1)}), bf16[128,16,2560]{2,1,0:T(8,128)(2,1)}, u32[]{:S(2)}, u32[]{:S(2)}) %all-to-all-start.1) | async-done | bytes 10485792 | tf_op jit(solution)/shard_map/all_to_all | solution.py:140
  1066.7 19.8 %all-to-all-start.3 = ((bf16[8,16,256]{2,1,0:T(8,128)(2,1)}), bf16[8,16,256]{2,1,0:T(8,128)(2,1)S(1)}, u32[]{:S(2)}, u32[]{:S(2)}) async-start(bf16[8,16,256]{2,1,0:T(8,128)(2,1)} %convert_element_type.104), calls=%async_computation.3 | async-start | bytes 131072 | tf_op jit(solution)/shard_map/all_to_all | solution.py:157
  1086.5 14.1 %convert.14 = f32[64,2,16,2560]{3,2,1,0:T(8,128)} convert(bf16[64,2,16,2560]{3,2,1,0:T(8,128)(2,1)} %bitcast.24) | non-fusion elementwise | flops 5242880 | bytes 31457280 | tf_op jit(solution)/shard_map/convert_element_type | solution.py:143
  1100.5 11.1 fusion.1
  1111.6 11.5 gather_fusion.2
  1123.1 7.8 reshape.307
  1130.9 8.0 multiply_reduce_fusion
  1139.0 5.2 all-to-all-start.4
  1144.1 1.0 add_convert_fusion
  1145.1 4.2 all-to-all-done.4
  1149.3 3.5 all-to-all-start.2
  1153.1 1.0 gather_fusion
  1154.1 1.6 scatter_custom_fusion.2
  1155.7 1.6 scatter_custom_fusion.3
  1157.3 5.8 all-to-all-done.2
  1163.1 2.4 scatter_custom_fusion.1
  (54 shorter events, 2.5 us)
Async XLA Ops:
  7.2 323.5 %all-gather.7.cloned.1.call-start = ((), (), s32[]{:S(2)}) async-start(), calls=%async_computation.6 | async-start | bytes 10567680 | tf_op jit(solution)/shard_map/all_gather | solution.py:76
  7.9 643.8 %all-gather.5.cloned.1.call-start = ((), (), s32[]{:S(2)}) async-start(), calls=%async_computation.5 | async-start | bytes 11096064 | tf_op jit(solution)/shard_map/all_gather | solution.py:75
  343.4 321.4 %copy-start.1 = (bf16[128,2560]{1,0:T(8,128)(2,1)S(1)}, bf16[128,2560]{1,0:T(8,128)(2,1)}, u32[]{:S(2)}) copy-start(bf16[128,2560]{1,0:T(8,128)(2,1)} %param.11) | copy-start | bytes 1966084
  343.4 321.4 %copy-start.2 = (f32[2560]{0:T(1024)S(1)}, f32[2560]{0:T(1024)}, u32[]{:S(2)}) copy-start(f32[2560]{0:T(1024)} %param.14) | copy-start | bytes 30724
  717.6 2.3 slice-start
  718.7 2.3 slice-start.1
  721.0 1.1 copy-start.3
  873.3 21.6 %copy-start.5 = (bf16[1,768,2560]{2,1,0:T(8,128)(2,1)S(1)}, bf16[1,768,2560]{2,1,0:T(8,128)(2,1)}, u32[]{:S(2)}) copy-start(bf16[1,768,2560]{2,1,0:T(8,128)(2,1)} %param.21) | copy-start | bytes 11796484
  912.2 12.1 %copy-start.4 = (f32[128,6]{0,1:T(8,128)S(1)}, f32[128,6]{0,1:T(8,128)}, u32[]{:S(2)}) copy-start(f32[128,6]{0,1:T(8,128)} %param.19) | copy-start | bytes 9220
  912.2 154.5 %all-to-all-start.1 = ((bf16[128,16,2560]{2,1,0:T(8,128)(2,1)}), bf16[128,16,2560]{2,1,0:T(8,128)(2,1)}, u32[]{:S(2)}, u32[]{:S(2)}) async-start(bf16[128,16,2560]{2,1,0:T(8,128)(2,1)} %bitcast.109), calls=%async_computation.1 | async-start | bytes 20971520 | tf_op jit(solution)/shard_map/all_to_all | solution.py:140
  1066.7 72.3 %all-to-all-start.3 = ((bf16[8,16,256]{2,1,0:T(8,128)(2,1)}), bf16[8,16,256]{2,1,0:T(8,128)(2,1)S(1)}, u32[]{:S(2)}, u32[]{:S(2)}) async-start(bf16[8,16,256]{2,1,0:T(8,128)(2,1)} %convert_element_type.104), calls=%async_computation.3 | async-start | bytes 131072 | tf_op jit(solution)/shard_map/all_to_all | solution.py:157
  1130.9 22.1 %copy-start = (s32[1024]{0:T(1024)S(1)}, s32[1024]{0:T(1024)}, u32[]{:S(2)}) copy-start(s32[1024]{0:T(1024)} %param.12) | copy-start | bytes 12292
  1139.0 10.4 all-to-all-start.4
  1149.3 13.7 %all-to-all-start.2 = ((bf16[8,16,2560]{2,1,0:T(8,128)(2,1)}), bf16[8,16,2560]{2,1,0:T(8,128)(2,1)S(1)}, u32[]{:S(2)}, u32[]{:S(2)}) async-start(bf16[8,16,2560]{2,1,0:T(8,128)(2,1)} %bitcast.26), calls=%async_computation.2 | async-start | bytes 1310720 | tf_op jit(solution)/shard_map/all_to_all | solution.py:156
Sparse Core Ops, SparseCore 0:
  9.7 320.9 all-gather.6
  332.3 319.3 all-gather.4
where the time goes:
time: 1180 us; the launch traced here: 1170 us
  waiting for transfers between devices  772 us (65%)
  blocking collectives  181 us (15%)
  local copies, waits for them, and re-layouts  74.5 us (6%)
  matrix products  47.2 us (4%)
  other arithmetic  42 us (4%)
  starting transfers between devices  40.6 us (3%)
  between operations  14.4 us (1%)
    all_gather x1, waiting for transfers between devices, per_device(): lax.all_gather(w_out, ('dp', 'cache'), axis=0, tiled=True)  311 us
    all_gather x1, waiting for transfers between devices, per_device(): lax.all_gather(w_qkv, ('dp', 'cache'), axis=0, tiled=True)  308 us
    all_to_all x1, waiting for transfers between devices, per_device(): lax.all_to_all(partial_value, ('dp', 'cache'), split_axis=0, concat_axis=...  142 us
    all_to_all x1, blocking collectives, per_device(): lax.all_to_all(jnp.repeat(outgoing, 2, axis=0), ('dp', 'cache'), split_ax...  137 us
    unnamed x20, local copies, waits for them, and re-layouts  28.1 us
  transfers between devices with their start and end apart: 6, of which 5 were waited for; matrix products, arithmetic and copies ran while one was open for 7% of the time, Pallas kernels for 0%

commit v1 on v0

--- a/solution.py
+++ b/solution.py
@@ -72,7 +72,12 @@
     position = my_place - prompt_start
     normed = rms_scaled(hidden_in, attn_gain)
     full_qkv, full_out = (
-        lax.all_gather(w_qkv, ("dp", "cache"), axis=0, tiled=True),
+        jnp.concatenate(
+            lax.all_to_all(
+                jnp.stack(lax.axis_size(("dp", "cache")) * [w_qkv], 0), ("dp", "cache"), 0, 0
+            ),
+            0,
+        ),
         lax.all_gather(w_out, ("dp", "cache"), axis=0, tiled=True),
     )
     projected = jnp.dot(normed, full_qkv, preferred_element_type=jnp.float32)

time: 1180 us -> 899 us (0.76)
  waiting for transfers between devices: 772 us -> 481 us
    all_gather x1 -> x0, waiting for transfers between devices: 308 us -> none  [per_device(): lax.all_gather(w_qkv, ('dp', 'cache'), axis=0, tiled=True)]
    all_to_all x0 -> x1, waiting for transfers between devices: none -> 149 us  [per_device(): lax.all_to_all(jnp.stack(lax.axis_size(('dp', 'cache')) * [w_qkv], 0), ('...]
    all_gather x1, waiting for transfers between devices: 311 us -> 180 us  [per_device(): lax.all_gather(w_out, ('dp', 'cache'), axis=0, tiled=True)]
    unnamed x20 -> x21, local copies, waits for them, and re-layouts: 28.1 us -> 13.1 us
    reshape x0 -> x1, local copies, waits for them, and re-layouts: none -> 13.2 us  [per_device(): jnp.concatenate(lax.all_to_all(jnp.stack(lax.axis_size(('dp', 'cache')) *...]
  transfers between devices with their start and end apart: 6 -> 6, of which waited for: 5 -> 5; matrix products, arithmetic and copies ran while one was open for 7% -> 11% of each run, Pallas kernels for 0% -> 0%
where the time goes in v1:
time: 899 us; the launch traced here: 893 us
  waiting for transfers between devices  481 us (54%)
  blocking collectives  189 us (21%)
  local copies, waits for them, and re-layouts  78.4 us (9%)
  matrix products  50.2 us (6%)
  starting transfers between devices  40.4 us (4%)
  other arithmetic  38.8 us (4%)
  between operations  14.6 us (2%)
    all_gather x1, waiting for transfers between devices, per_device(): lax.all_gather(w_out, ('dp', 'cache'), axis=0, tiled=True)  180 us
    all_to_all x1, waiting for transfers between devices, per_device(): lax.all_to_all(jnp.stack(lax.axis_size(('dp', 'cache')) * [w_qkv], 0), ('...  149 us
    all_to_all x1, waiting for transfers between devices, per_device(): lax.all_to_all(partial_value, ('dp', 'cache'), split_axis=0, concat_axis=...  142 us
    all_to_all x1, blocking collectives, per_device(): lax.all_to_all(jnp.repeat(outgoing, 2, axis=0), ('dp', 'cache'), split_ax...  133 us
    all_gather x1, blocking collectives, per_device(): value_piece = lax.all_gather(values_here, 'cache', axis=0, tiled=True)  30.3 us
    all_gather x1, blocking collectives, per_device(): key_piece = lax.all_gather(keys_here, 'cache', axis=0, tiled=True)  25.3 us
    dot_general x1, matrix products, expert_half(): joined = jnp.dot(flat_rows, gate_up, preferred_element_type=jnp.float32)  21.6 us
  transfers between devices with their start and end apart: 6, of which 5 were waited for; matrix products, arithmetic and copies ran while one was open for 11% of the time, Pallas kernels for 0%

profile of v1, /device:TPU:33, one launch (start us, length us, event | category | flops | bytes accessed | tf_op | source)
XLA Modules:
  0.0 892.6 jit_solution(5542672520479882659)
XLA Ops:
  7.2 0.7 all-gather.3.cloned.1.call-update
  7.9 5.7 stack.2
  13.6 10.9 %all-to-all-start = ((bf16[128,20,1792]{2,1,0:T(8,128)(2,1)}), bf16[128,20,1792]{2,1,0:T(8,128)(2,1)}, u32[]{:S(2)}, u32[]{:S(2)}) async-start(bf16[128,20,1792]{2,1,0:T(8,128)(2,1)} %stack.2), calls=%async_computation | async-start | bytes 22020096 | tf_op jit(solution)/shard_map/all_to_all | solution.py:76
  25.1 0.2 multiply_cosine_fusion
  25.8 1.8 reduce-window.6
  27.6 0.3 slice_reduce_fusion
  28.1 3.4 scatter_custom_fusion
  31.5 0.2 fusion.18
  31.7 0.2 compare_and_fusion
  31.9 148.7 %all-to-all-done = bf16[128,20,1792]{2,1,0:T(8,128)(2,1)} async-done(((bf16[128,20,1792]{2,1,0:T(8,128)(2,1)}), bf16[128,20,1792]{2,1,0:T(8,128)(2,1)}, u32[]{:S(2)}, u32[]{:S(2)}) %all-to-all-start) | async-done | bytes 9175072 | tf_op jit(solution)/shard_map/all_to_all | solution.py:76
  180.6 13.2 %reshape.297 = bf16[2560,1792]{1,0:T(8,128)(2,1)} reshape(bf16[128,20,1792]{2,1,0:T(8,128)(2,1)} %all-to-all-done) | data formatting | bytes 18350080 | tf_op jit(solution)/shard_map/reshape | solution.py:75
  193.8 5.1 fusion.30
  198.9 0.6 slice.95
  199.6 30.3 %all_gather.9 = bf16[1024,256]{1,0:T(8,128)(2,1)S(1)} all-gather(bf16[128,256]{1,0:T(8,128)(2,1)} %slice.95), channel_id=1, replica_groups=mesh['dp'=16,'cache'=8] {'cache'}, dimensions={0}, use_global_device_ids=true | all-gather | bytes 589824 | tf_op jit(solution)/shard_map/all_gather | solution.py:92
  229.9 0.2 copy.53
  230.2 0.3 multiply_subtract_fusion
  230.5 0.2 maximum_convert_fusion
  230.8 0.2 copy.38
  231.2 25.3 %all_gather.10 = bf16[1024,256]{0,1:T(8,128)(2,1)S(1)} all-gather(bf16[128,256]{0,1:T(8,128)(2,1)S(1)} %bitcast.114), channel_id=1, replica_groups=mesh['dp'=16,'cache'=8] {'cache'}, dimensions={0}, use_global_device_ids=true | all-gather | bytes 589824 | tf_op jit(solution)/shard_map/all_gather | solution.py:91
  256.5 1.0 fusion.5
  257.5 1.1 fusion.8
  258.6 1.2 fusion.27
  259.8 180.4 %all-gather.3.cloned.1.call-done = bf16[128,10,2560]{2,1,0:T(8,128)(2,1)} async-done(((bf16[1,10,2560]{2,1,0:T(8,128)(2,1)}), bf16[128,10,2560]{2,1,0:T(8,128)(2,1)}) %all-gather.3.cloned.1.call-update) | async-done | bytes 6553616 | tf_op jit(solution)/shard_map/all_gather | solution.py:81
  440.2 12.8 %reshape.372 = bf16[1280,2560]{1,0:T(8,128)(2,1)} reshape(bf16[128,10,2560]{2,1,0:T(8,128)(2,1)} %all-gather.3.cloned.1.call-done) | data formatting | bytes 13107200
  453.0 4.0 multiply_reduce_fusion.1
  457.3 6.3 gather_fusion.1
  463.6 7.8 broadcast_in_dim.35
  471.4 133.0 %all_to_all.30 = bf16[128,16,2560]{2,1,0:T(8,128)(2,1)S(1)} all-to-all(bf16[128,16,2560]{2,1,0:T(8,128)(2,1)} %bitcast.104), channel_id=1, replica_groups=mesh['dp'=16,'cache'=8] {'dp','cache'}, dimensions={0} | all-to-all | bytes 20971520 | tf_op jit(solution)/shard_map/all_to_all | solution.py:135
  604.4 21.6 %fusion.2 = f32[2048,1536]{1,0:T(8,128)} fusion(bf16[2048,2560]{1,0:T(8,128)(2,1)S(1)} %bitcast.107, bf16[1,2560,1536]{2,1,0:T(8,128)(2,1)} %param.20), kind=kOutput, calls=%fused_computation.13 | convolution fusion | flops 16106127360 | bytes 30932992 | tf_op jit(solution)/shard_map/dot_general | solution.py:40
  626.0 17.3 %convolution_convert_fusion = bf16[2048,2560]{1,0:T(8,128)(2,1)} fusion(bf16[1,768,2560]{2,1,0:T(8,128)(2,1)S(1)} %copy-done.8, f32[2048,1536]{1,0:T(8,128)} %fusion.2), kind=kOutput, calls=%fused_computation.7 | convolution fusion | flops 8067743744 | bytes 27000832 | tf_op jit(solution)/shard_map/dot_general | solution.py:44
  643.3 10.4 %all-to-all-start.2 = ((bf16[128,16,2560]{2,1,0:T(8,128)(2,1)}), bf16[128,16,2560]{2,1,0:T(8,128)(2,1)}, u32[]{:S(2)}, u32[]{:S(2)}) async-start(bf16[128,16,2560]{2,1,0:T(8,128)(2,1)} %bitcast.106), calls=%async_computation.2 | async-start | bytes 20971520 | tf_op jit(solution)/shard_map/all_to_all | solution.py:145
  653.9 0.7 convert_element_type.104
  654.6 141.6 %all-to-all-done.2 = bf16[128,16,2560]{2,1,0:T(8,128)(2,1)} async-done(((bf16[128,16,2560]{2,1,0:T(8,128)(2,1)}), bf16[128,16,2560]{2,1,0:T(8,128)(2,1)}, u32[]{:S(2)}, u32[]{:S(2)}) %all-to-all-start.2) | async-done | bytes 10485792 | tf_op jit(solution)/shard_map/all_to_all | solution.py:145
  796.2 10.3 %all-to-all-start.4 = ((bf16[8,16,256]{2,1,0:T(8,128)(2,1)}), bf16[8,16,256]{2,1,0:T(8,128)(2,1)S(1)}, u32[]{:S(2)}, u32[]{:S(2)}) async-start(bf16[8,16,256]{2,1,0:T(8,128)(2,1)} %convert_element_type.104), calls=%async_computation.4 | async-start | bytes 131072 | tf_op jit(solution)/shard_map/all_to_all | solution.py:162
  806.6 14.1 %convert.14 = f32[64,2,16,2560]{3,2,1,0:T(8,128)} convert(bf16[64,2,16,2560]{3,2,1,0:T(8,128)(2,1)} %bitcast.23) | non-fusion elementwise | flops 5242880 | bytes 31457280 | tf_op jit(solution)/shard_map/convert_element_type | solution.py:148
  820.6 11.1 %fusion.1 = bf16[64,1,16,2560]{3,2,0,1:T(8,128)(2,1)} fusion(f32[64,2,16,2560]{3,2,1,0:T(8,128)} %convert.14), kind=kLoop, calls=%fused_computation.10 | loop fusion | flops 5242880 | bytes 26214400 | tf_op jit(solution)/shard_map/convert_element_type | solution.py:149
  831.7 11.5 %gather_fusion.2 = bf16[768,2560]{1,0:T(8,128)(2,1)} fusion(bf16[1024,2560]{1,0:T(8,128)(2,1)} %bitcast.103, s32[1024]{0:T(1024)S(1)} %pad_clamp_fusion), kind=kCustom, calls=%fused_computation.2 | custom fusion | bytes 7867392 | tf_op jit(solution)/shard_map/gather | solution.py:150
  843.2 7.8 reshape.313
  851.0 8.0 multiply_reduce_fusion
  859.1 5.2 all-to-all-start.5
  864.2 1.0 add_convert_fusion
  865.2 4.2 all-to-all-done.5
  869.4 3.5 all-to-all-start.3
  873.1 1.0 gather_fusion
  874.1 1.6 scatter_custom_fusion.2
  875.7 1.6 scatter_custom_fusion.3
  877.4 5.8 all-to-all-done.3
  883.2 2.4 scatter_custom_fusion.1
  (55 shorter events, 2.1 us)
Async XLA Ops:
  7.2 433.0 %all-gather.3.cloned.1.call-start = ((), (), s32[]{:S(2)}) async-start(), calls=%async_computation.6 | async-start | bytes 10567680 | tf_op jit(solution)/shard_map/all_gather | solution.py:81
  13.6 11.0 %copy-start.4 = (s32[128,6]{0,1:T(8,128)S(1)}, s32[128,6]{0,1:T(8,128)}, u32[]{:S(2)}) copy-start(s32[128,6]{0,1:T(8,128)} %param.18) | copy-start | bytes 9220
  13.6 11.4 %copy-start = (s32[1024]{0:T(1024)S(1)}, s32[1024]{0:T(1024)}, u32[]{:S(2)}) copy-start(s32[1024]{0:T(1024)} %param.12) | copy-start | bytes 12292
  13.6 11.4 %copy-start.7 = (s32[128]{0:T(128)S(1)}, s32[128]{0:T(128)}, u32[]{:S(2)}) copy-start(s32[128]{0:T(128)} %param.13) | copy-start | bytes 1540
  13.6 17.8 %copy-start.2 = (bf16[128,2560]{1,0:T(8,128)(2,1)S(1)}, bf16[128,2560]{1,0:T(8,128)(2,1)}, u32[]{:S(2)}) copy-start(bf16[128,2560]{1,0:T(8,128)(2,1)} %param.11) | copy-start | bytes 1966084
  13.6 167.0 %all-to-all-start = ((bf16[128,20,1792]{2,1,0:T(8,128)(2,1)}), bf16[128,20,1792]{2,1,0:T(8,128)(2,1)}, u32[]{:S(2)}, u32[]{:S(2)}) async-start(bf16[128,20,1792]{2,1,0:T(8,128)(2,1)} %stack.2), calls=%async_computation | async-start | bytes 22020096 | tf_op jit(solution)/shard_map/all_to_all | solution.py:76
  31.9 161.9 %copy-start.3 = (f32[2560]{0:T(1024)S(1)}, f32[2560]{0:T(1024)}, u32[]{:S(2)}) copy-start(f32[2560]{0:T(1024)} %param.14) | copy-start | bytes 30724
  453.0 4.0 copy-start.5
  604.4 21.6 %copy-start.8 = (bf16[1,768,2560]{2,1,0:T(8,128)(2,1)S(1)}, bf16[1,768,2560]{2,1,0:T(8,128)(2,1)}, u32[]{:S(2)}) copy-start(bf16[1,768,2560]{2,1,0:T(8,128)(2,1)} %param.21) | copy-start | bytes 11796484
  643.3 10.4 %copy-start.6 = (f32[128,6]{0,1:T(8,128)S(1)}, f32[128,6]{0,1:T(8,128)}, u32[]{:S(2)}) copy-start(f32[128,6]{0,1:T(8,128)} %param.19) | copy-start | bytes 9220
  643.3 152.9 %all-to-all-start.2 = ((bf16[128,16,2560]{2,1,0:T(8,128)(2,1)}), bf16[128,16,2560]{2,1,0:T(8,128)(2,1)}, u32[]{:S(2)}, u32[]{:S(2)}) async-start(bf16[128,16,2560]{2,1,0:T(8,128)(2,1)} %bitcast.106), calls=%async_computation.2 | async-start | bytes 20971520 | tf_op jit(solution)/shard_map/all_to_all | solution.py:145
  796.2 62.8 %all-to-all-start.4 = ((bf16[8,16,256]{2,1,0:T(8,128)(2,1)}), bf16[8,16,256]{2,1,0:T(8,128)(2,1)S(1)}, u32[]{:S(2)}, u32[]{:S(2)}) async-start(bf16[8,16,256]{2,1,0:T(8,128)(2,1)} %convert_element_type.104), calls=%async_computation.4 | async-start | bytes 131072 | tf_op jit(solution)/shard_map/all_to_all | solution.py:162
  851.0 22.1 %copy-start.1 = (s32[1024]{0:T(1024)S(1)}, s32[1024]{0:T(1024)}, u32[]{:S(2)}) copy-start(s32[1024]{0:T(1024)} %param.12) | copy-start | bytes 12292
  859.1 10.4 %all-to-all-start.5 = ((bf16[8,16,256]{2,1,0:T(8,128)(2,1)}), bf16[8,16,256]{2,1,0:T(8,128)(2,1)S(1)}, u32[]{:S(2)}, u32[]{:S(2)}) async-start(bf16[8,16,256]{2,1,0:T(8,128)(2,1)} %bitcast.28), calls=%async_computation.5 | async-start | bytes 131072 | tf_op jit(solution)/shard_map/all_to_all | solution.py:163
  869.4 13.7 %all-to-all-start.3 = ((bf16[8,16,2560]{2,1,0:T(8,128)(2,1)}), bf16[8,16,2560]{2,1,0:T(8,128)(2,1)S(1)}, u32[]{:S(2)}, u32[]{:S(2)}) async-start(bf16[8,16,2560]{2,1,0:T(8,128)(2,1)} %bitcast.25), calls=%async_computation.3 | async-start | bytes 1310720 | tf_op jit(solution)/shard_map/all_to_all | solution.py:161
Sparse Core Ops, SparseCore 0:
  9.7 430.4 all-gather.2
